TPU v7x, 256 devices: a whole 4x4x8 slice. The times are simulated.
256 devices in a mesh: ia: 4 (over y), ja: 4 (over x), ka: 16 (over z, core).
Axes of the slice: x: 4, y: 4, z: 8, core: 2. Of those that a mesh axis runs over, the one named last changes fastest.
Arguments:
- blocks: bfloat16 [4, 4, 16, 2, 128, 128, 128], P('ia', 'ja', 'ka'), may hold values from -6 to 6
- first_mode_rows: int32 [4, 4, 16, 2], P('ia', 'ja', 'ka'), may hold values from 0 to 15
- second_mode_rows: int32 [4, 4, 16, 2], P('ia', 'ja', 'ka'), may hold values from 0 to 15
- third_mode_rows: int32 [4, 4, 16, 2], P('ia', 'ja', 'ka'), may hold values from 0 to 3
- filled: int32 [4, 4, 16], P('ia', 'ja', 'ka'), may hold values from 1 to 2, as said below
- owner_one: int32 [64], replicated, may hold values from 0 to 63, each once
- owner_two: int32 [64], replicated, may hold values from 0 to 63, each once
- factor_b: float32 [4, 2048, 256], P('ja', ('ia', 'ka'))
- factor_c: float32 [16, 512, 256], P('ka')
Outputs:
- a_new: float32 [4, 2048, 256], P('ia', ('ja', 'ka'))
- b_new: float32 [4, 2048, 256], P('ja', ('ia', 'ka'))
Inputs may be any that keep to these rules, and one draw needn't show every extreme that they name: Number of nonempty slots of a grid cell; at least one cell has all 2 slots filled. Slots at or beyond this count hold data that is not part of the tensor.
All inputs are finite; a program needn't handle non-finite values.
Results may differ from a plain program's by a relative error of at most 0.0039.
The roundings to bfloat16 on the way count: a program that leaves them out, or rounds other values in their place, can miss the bound.
Values may be sent and summed in bfloat16 or wider, within the bound.
A program may use at most 128 MiB of HBM per device.

v0:
```python
import jax
import jax.numpy as jnp
from jax import lax
from jax.sharding import PartitionSpec as P

EPS = 1e-06


def solve_rows(gram, rows):
    lower = jnp.linalg.cholesky(gram)
    return jax.scipy.linalg.cho_solve((lower, True), rows.T).T


def add_rows(accum, start, contrib):
    current = lax.dynamic_slice_in_dim(accum, start, contrib.shape[0], 0)
    return lax.dynamic_update_slice_in_dim(accum, current + contrib, start, 0)


def batched_sum(inner, weights):
    summed = lax.dot_general(
        inner,
        weights.astype(jnp.float32),
        (((1,), (0,)), ((2,), (1,))),
        precision=lax.Precision.HIGHEST,
        preferred_element_type=jnp.float32,
    )
    return summed.T


def to_logical(stored, owner, piece_rows):
    return stored.reshape(-1, piece_rows, stored.shape[1])[owner].reshape(stored.shape)


def to_stored(logical, owner, piece_rows):
    positions = jnp.arange(owner.shape[0], dtype=jnp.int32)
    inverse = jnp.sum(
        jnp.where(owner[None, :] == positions[:, None], positions[None, :], 0), axis=1
    )
    return logical.reshape(-1, piece_rows, logical.shape[1])[inverse].reshape(logical.shape)


def keep_same(value):
    return value


def partial_value(function, slot):

    def applied(value):
        return function(value, slot)

    return applied


def body(
    blocks,
    first_mode_rows,
    second_mode_rows,
    third_mode_rows,
    filled,
    owner_one,
    owner_two,
    factor_b,
    factor_c,
):
    highest = lax.Precision.HIGHEST
    piece_rows = factor_b.shape[1]
    rank_width = factor_b.shape[2]
    block_edge = blocks.shape[-1]
    slot_count = blocks.shape[3]
    total_one = piece_rows * lax.axis_size("ia") * lax.axis_size("ja") * lax.axis_size("ka")
    slab_rows_one = piece_rows * lax.axis_size("ja") * lax.axis_size("ka")
    slab_rows_two = piece_rows * lax.axis_size("ia") * lax.axis_size("ka")
    own_b = factor_b[0]
    own_c = lax.dynamic_slice_in_dim(
        factor_c[0], lax.axis_index(("ia", "ja")) * piece_rows, piece_rows, 0
    )
    local_b = jnp.dot(own_b.T, own_b, precision=highest, preferred_element_type=jnp.float32)
    local_c = jnp.dot(own_c.T, own_c, precision=highest, preferred_element_type=jnp.float32)
    gram_b, gram_c = lax.psum((local_b, local_c), ("ia", "ja", "ka"))
    stored_b = lax.all_gather(factor_b.astype(jnp.bfloat16), ("ia", "ka"), axis=1, tiled=True)[0]
    half_b = to_logical(stored_b, owner_two, piece_rows)
    half_c = factor_c[0].astype(jnp.bfloat16)
    live_count = filled[0, 0, 0]

    def update_one(partial_sum, slot):
        block = blocks[0, 0, 0, slot]
        b_rows = lax.dynamic_slice_in_dim(
            half_b, second_mode_rows[0, 0, 0, slot] * block_edge, block_edge, 0
        )
        c_rows = lax.dynamic_slice_in_dim(
            half_c, third_mode_rows[0, 0, 0, slot] * block_edge, block_edge, 0
        )
        inner = jnp.dot(
            block.reshape(block_edge * block_edge, block_edge),
            c_rows,
            preferred_element_type=jnp.float32,
        )
        inner = inner.reshape(block_edge, block_edge, rank_width)
        contrib = batched_sum(inner, b_rows)
        return add_rows(partial_sum, first_mode_rows[0, 0, 0, slot] * block_edge, contrib)

    partial_one = jnp.zeros((slab_rows_one, rank_width), jnp.float32)
    for slot in range(slot_count):
        partial_one = lax.cond(
            slot < live_count, partial_value(update_one, slot), keep_same, partial_one
        )
    stored_one = to_stored(partial_one, owner_one, piece_rows)
    system_one = gram_b * gram_c
    summed_own = lax.psum_scatter(stored_one, ("ja", "ka"), scatter_dimension=0, tiled=True)
    a_hat = solve_rows(system_one, summed_own)
    squares_a = lax.psum(jnp.sum(a_hat * a_hat, axis=0), ("ia", "ja", "ka"))
    scale_a = jnp.sqrt(squares_a / total_one + EPS)
    a_own = a_hat / scale_a
    local_a = jnp.dot(a_own.T, a_own, precision=highest, preferred_element_type=jnp.float32)
    gram_a = lax.psum(local_a, ("ia", "ja", "ka"))
    stored_a = lax.all_gather(a_own.astype(jnp.bfloat16)[None], ("ja", "ka"), axis=1, tiled=True)[0]
    half_a = to_logical(stored_a, owner_one, piece_rows)

    def update_two(partial_sum, slot):
        block = blocks[0, 0, 0, slot]
        a_rows = lax.dynamic_slice_in_dim(
            half_a, first_mode_rows[0, 0, 0, slot] * block_edge, block_edge, 0
        )
        c_rows = lax.dynamic_slice_in_dim(
            half_c, third_mode_rows[0, 0, 0, slot] * block_edge, block_edge, 0
        )
        inner = lax.dot_general(
            block.reshape(block_edge, block_edge * block_edge),
            a_rows,
            (((0,), (0,)), ((), ())),
            preferred_element_type=jnp.float32,
        )
        inner = inner.reshape(block_edge, block_edge, rank_width)
        contrib = batched_sum(inner, c_rows)
        return add_rows(partial_sum, second_mode_rows[0, 0, 0, slot] * block_edge, contrib)

    partial_two = jnp.zeros((slab_rows_two, rank_width), jnp.float32)
    for slot in range(slot_count):
        partial_two = lax.cond(
            slot < live_count, partial_value(update_two, slot), keep_same, partial_two
        )
    stored_two = to_stored(partial_two, owner_two, piece_rows)
    summed_two = lax.psum_scatter(stored_two, ("ia", "ka"), scatter_dimension=0, tiled=True)
    b_hat = solve_rows(gram_a * gram_c, summed_two)
    squares_b = lax.psum(jnp.sum(b_hat * b_hat, axis=0), ("ia", "ja", "ka"))
    b_own = b_hat / jnp.sqrt(squares_b / total_one + EPS)
    return (a_own[None], b_own[None])


def solution(mesh):
    return jax.shard_map(
        body,
        mesh=mesh,
        in_specs=(
            P("ia", "ja", "ka", None, None, None, None),
            P("ia", "ja", "ka", None),
            P("ia", "ja", "ka", None),
            P("ia", "ja", "ka", None),
            P("ia", "ja", "ka"),
            P(),
            P(),
            P("ja", ("ia", "ka"), None),
            P("ka", None, None),
        ),
        out_specs=(P("ia", ("ja", "ka"), None), P("ja", ("ia", "ka"), None)),
        check_vma=False,
    )
```

profile of v0, /device:TPU:1, one launch (start us, length us, event | category | flops | bytes accessed | tf_op | source)
XLA Modules:
  0.0 827.5 jit_solution(4852424667202017735)
XLA Ops:
  17.5 75.5 %all-gather.4.cloned.1.call-done = bf16[1,2048,256]{2,1,0:T(8,128)(2,1)} async-done(((bf16[1,32,256]{2,1,0:T(8,128)(2,1)}), bf16[1,2048,256]{2,1,0:T(8,128)(2,1)}) %all-gather.4.cloned.1.call-update) | async-done | bytes 1048592 | tf_op jit(solution)/shard_map/all_gather | solution.py:80
  94.8 23.3 %conditional.4 = (f32[2048,256]{1,0:T(8,128)}) conditional(s32[]{:T(128)} %bitcast.41, () %tuple.54, (s32[1,1,1,2]{3,2,1,0:T(1,128)}, bf16[512,256]{1,0:T(8,128)(2,1)S(1)}, bf16[1,1,1,2,128,128,128]{6,5,4,3,2,1,0:T(8,128)(2,1)}, s32[1,1,1,2]{3,2,1,0:T(1,128)}, bf16[2048,256]{1,0:T(8,128)(2,1)S(1)}, /*index=5*/s32[1,1,1,2]{3,2,1,0:T(1,128)}) %tuple.134), branch_computations={%region_6.0_spmd, %region_7.0_spmd} | conditional | flops 1082130432 | bytes 83099928 | solution.py:104
  100.7 6.7 copy.52
  107.6 8.2 multiply_reduce_fusion
  118.1 3.6 gather_fusion.1
  122.1 149.6 %all-reduce.7.cloned.1.call-done = (f32[256,256]{0,1:T(8,128)}, f32[256,256]{0,1:T(8,128)}) async-done(((f32[256,256]{0,1:T(8,128)}, f32[256,256]{0,1:T(8,128)}), (f32[256,256]{0,1:T(8,128)}, f32[256,256]{0,1:T(8,128)})) %all-reduce.7.cloned.1.call-update) | async-done | bytes 524304 | tf_op jit(solution)/shard_map/psum | solution.py:79
  272.9 11.7 %cholesky.130 = f32[128,128]{1,0:T(8,128)S(1)} custom-call(f32[128,128]{1,0:T(8,128)S(1)} %cholesky.194), custom_call_target="Cholesky" | custom-call | tf_op jit(solution)/shard_map/jit(cholesky)/cholesky | solution.py:10
  284.7 9.8 %custom-call.15 = f32[1,128,128]{1,2,0:T(8,128)S(1)} custom-call(f32[1,128,128]{2,1,0:T(8,128)S(1)} %get-tuple-element.155), custom_call_target="InvertDiagBlocksLowerTriangular" | custom-call | tf_op jit(solution)/shard_map/jit(cholesky)/cholesky | solution.py:10
  295.0 11.7 %cholesky.147 = f32[128,128]{1,0:T(8,128)S(1)} custom-call(f32[128,128]{1,0:T(8,128)S(1)} %convolution_subtract_fusion.1), custom_call_target="Cholesky" | custom-call | tf_op jit(solution)/shard_map/jit(cholesky)/cholesky | solution.py:10
  308.8 14.6 %while.4 = (s32[]{:T(128)}, f32[256,256]{1,0:T(8,128)S(1)}, s32[2,2]{1,0:T(2,128)S(1)}, f32[2,128,128]{2,1,0:T(8,128)S(1)}, s32[]{:T(128)}) while((s32[]{:T(128)}, f32[256,256]{1,0:T(8,128)S(1)}, s32[2,2]{1,0:T(2,128)S(1)}, f32[2,128,128]{2,1,0:T(8,128)S(1)}, s32[]{:T(128)}) %tuple.103), condition=%wide.while_cond, body=%wide.while_body.sunk | while | flops 2 | bytes 131181 | solution.py:11
  323.4 19.7 %custom-call.16 = f32[2,128,128]{1,2,0:T(8,128)S(1)} custom-call(f32[2,128,128]{2,1,0:T(8,128)S(1)} %get-tuple-element.124), custom_call_target="InvertDiagBlocksLowerTriangular" | custom-call | tf_op jit(solution)/shard_map/jit(_cho_solve)/triangular_solve | solution.py:11
  345.9 77.9 %psum.37 = f32[256]{0:T(256)S(1)} all-reduce(f32[256]{0:T(256)S(1)} %multiply_reduce_fusion.5), channel_id=1, replica_groups=mesh['ia'=4,'ja'=4,'ka'=16] {'ia','ja','ka'}, use_global_device_ids=true, to_apply=%region_13.16 | all-reduce | flops 256 | bytes 2048 | tf_op jit(solution)/shard_map/psum | solution.py:111
  425.8 71.7 %all-gather.6.cloned.1.call-done = bf16[2048,256]{1,0:T(8,128)(2,1)} async-done(((bf16[32,256]{1,0:T(8,128)(2,1)}), bf16[2048,256]{1,0:T(8,128)(2,1)}) %all-gather.6.cloned.1.call-update) | async-done | bytes 1048592 | tf_op jit(solution)/shard_map/all_gather | solution.py:116
  499.4 23.6 %conditional.6 = (f32[2048,256]{1,0:T(8,128)}) conditional(s32[]{:T(128)} %bitcast.41, () %tuple.57, (s32[1,1,1,2]{3,2,1,0:T(1,128)S(1)}, bf16[2048,256]{1,0:T(8,128)(2,1)S(1)}, bf16[1,1,1,2,128,128,128]{6,5,4,3,2,1,0:T(8,128)(2,1)}, s32[1,1,1,2]{3,2,1,0:T(1,128)S(1)}, bf16[512,256]{1,0:T(8,128)(2,1)S(1)}, ...), branch_computations={%region_15.18_spmd, %region_16.19_spmd} | conditional | flops 1082130432 | bytes 83099800 | solution.py:139
  505.5 6.7 copy.55
  512.4 8.3 multiply_reduce_fusion.2
  523.1 3.7 gather_fusion.3
  526.8 150.8 %all-reduce.5.cloned.1.call-done = f32[256,256]{0,1:T(8,128)} async-done(((f32[256,256]{0,1:T(8,128)}), f32[256,256]{0,1:T(8,128)}) %all-reduce.5.cloned.1.call-update) | async-done | bytes 262160 | tf_op jit(solution)/shard_map/psum | solution.py:115
  678.8 11.7 %cholesky.164 = f32[128,128]{1,0:T(8,128)S(1)} custom-call(f32[128,128]{1,0:T(8,128)S(1)} %cholesky.197), custom_call_target="Cholesky" | custom-call | tf_op jit(solution)/shard_map/jit(cholesky)/cholesky | solution.py:10
  690.6 9.8 %custom-call.17 = f32[1,128,128]{1,2,0:T(8,128)S(1)} custom-call(f32[1,128,128]{2,1,0:T(8,128)S(1)} %get-tuple-element.151), custom_call_target="InvertDiagBlocksLowerTriangular" | custom-call | tf_op jit(solution)/shard_map/jit(cholesky)/cholesky | solution.py:10
  700.9 11.7 %cholesky.181 = f32[128,128]{1,0:T(8,128)S(1)} custom-call(f32[128,128]{1,0:T(8,128)S(1)} %convolution_subtract_fusion), custom_call_target="Cholesky" | custom-call | tf_op jit(solution)/shard_map/jit(cholesky)/cholesky | solution.py:10
  715.2 4.2 while.5
  719.4 19.7 %custom-call.18 = f32[2,128,128]{1,2,0:T(8,128)S(1)} custom-call(f32[2,128,128]{2,1,0:T(8,128)S(1)} %get-tuple-element.125), custom_call_target="InvertDiagBlocksLowerTriangular" | custom-call | tf_op jit(solution)/shard_map/jit(_cho_solve)/triangular_solve | solution.py:11
  742.0 77.3 %psum.39 = f32[256]{0:T(256)S(1)} all-reduce(f32[256]{0:T(256)S(1)} %multiply_reduce_fusion.4), channel_id=1, replica_groups=mesh['ia'=4,'ja'=4,'ka'=16] {'ia','ja','ka'}, use_global_device_ids=true, to_apply=%region_22.25 | all-reduce | flops 256 | bytes 2048 | tf_op jit(solution)/shard_map/psum | solution.py:145
  (117 shorter events, 50.5 us)
Async XLA Ops:
  8.0 85.0 %all-gather.4.cloned.1.call-start = ((), (), s32[]{:S(2)}) async-start(), calls=%async_computation.2 | async-start | bytes 1064960 | tf_op jit(solution)/shard_map/all_gather | solution.py:80
  9.4 262.2 %all-reduce.7.cloned.1.call-start = ((), (), s32[]{:S(2)}) async-start(), calls=%async_computation.7 | async-start | bytes 1048576 | tf_op jit(solution)/shard_map/psum | solution.py:79
  13.5 329.6 %reduce-scatter.3.cloned.1.call-start = ((), (), s32[]{:S(2)}) async-start(), calls=%async_computation.3 | async-start | bytes 2129920 | tf_op jit(solution)/shard_map/reduce_scatter | solution.py:109
  100.7 6.7 copy-start.4
  107.5 8.4 %copy-start.7 = (s32[1,1,1,2]{3,2,1,0:T(1,128)S(1)}, s32[1,1,1,2]{3,2,1,0:T(1,128)}, u32[]{:S(2)}) copy-start(s32[1,1,1,2]{3,2,1,0:T(1,128)} %get-tuple-element.85) | copy-start | bytes 28 | tf_op jit(solution)/shard_map/cond
  121.7 302.8 %copy-start.1 = (s32[64]{0:T(128)S(1)}, s32[64]{0:T(128)}, u32[]{:S(2)}) copy-start(s32[64]{0:T(128)} %param.25) | copy-start | bytes 772
  121.8 375.7 %all-gather.6.cloned.1.call-start = ((), (), s32[]{:S(2)}) async-start(), calls=%async_computation.6 | async-start | bytes 1064960 | tf_op jit(solution)/shard_map/all_gather | solution.py:116
  271.6 227.7 %copy-start.2 = (s32[1,1,1,2]{3,2,1,0:T(1,128)S(1)}, s32[1,1,1,2]{3,2,1,0:T(1,128)}, u32[]{:S(2)}) copy-start(s32[1,1,1,2]{3,2,1,0:T(1,128)} %param.23) | copy-start | bytes 28
  271.6 227.7 %copy-start.3 = (s32[1,1,1,2]{3,2,1,0:T(1,128)S(1)}, s32[1,1,1,2]{3,2,1,0:T(1,128)}, u32[]{:S(2)}) copy-start(s32[1,1,1,2]{3,2,1,0:T(1,128)} %param.22) | copy-start | bytes 28
  271.6 227.7 %copy-start.6 = (s32[1,1,1,2]{3,2,1,0:T(1,128)S(1)}, s32[1,1,1,2]{3,2,1,0:T(1,128)}, u32[]{:S(2)}) copy-start(s32[1,1,1,2]{3,2,1,0:T(1,128)} %param.21) | copy-start | bytes 28
  424.5 253.1 %all-reduce.5.cloned.1.call-start = ((), (), s32[]{:S(2)}) async-start(), calls=%async_computation.4 | async-start | bytes 524288 | tf_op jit(solution)/shard_map/psum | solution.py:115
  425.8 313.4 %reduce-scatter.5.cloned.1.call-start = ((), (), s32[]{:S(2)}) async-start(), calls=%async_computation.5 | async-start | bytes 2129920 | tf_op jit(solution)/shard_map/reduce_scatter | solution.py:143
  523.1 154.5 %copy-start = (f32[256,256]{0,1:T(8,128)S(1)}, f32[256,256]{0,1:T(8,128)}, u32[]{:S(2)}) copy-start(f32[256,256]{0,1:T(8,128)} %get-tuple-element.143) | copy-start | bytes 786436
Sparse Core Ops, SparseCore 0:
  12.2 80.7 all-gather.3
  121.9 159.1 reduce-scatter.2
  424.6 72.8 all-gather.5
  527.0 159.5 reduce-scatter.4
Sparse Core Ops, SparseCore 1:
  15.6 256.0 all-reduce.6
  431.3 246.2 all-reduce.4
where the time goes:
time: 837 us; the launch traced here: 827 us
  waiting for transfers between devices  448 us (54%)
  blocking collectives  155 us (19%)
  other arithmetic  133 us (16%)
  local copies, waits for them, and re-layouts  42.5 us (5%)
  between operations  19.3 us (2%)
  matrix products  17.4 us (2%)
  loops' own time  12.2 us (1%)
    psum x1, waiting for transfers between devices, body(): gram_a = lax.psum(local_a, ('ia', 'ja', 'ka'))  151 us
    psum x1, waiting for transfers between devices, body(): gram_b, gram_c = lax.psum((local_b, local_c), ('ia', 'ja', 'ka'))  150 us
    psum x1, blocking collectives, body(): squares_a = lax.psum(jnp.sum(a_hat * a_hat, axis=0), ('ia', 'ja', 'ka'))  77.9 us
    psum x1, blocking collectives, body(): squares_b = lax.psum(jnp.sum(b_hat * b_hat, axis=0), ('ia', 'ja', 'ka'))  77.3 us
    all_gather x1, waiting for transfers between devices, body(): lax.all_gather(factor_b.astype(jnp.bfloat16), ('ia', 'ka'), axis=1, tiled...  75.5 us
    all_gather x1, waiting for transfers between devices, body(): lax.all_gather(a_own.astype(jnp.bfloat16)[None], ('ja', 'ka'), axis=1, ti...  71.7 us
    another operation x13, other arithmetic, solve_rows(): lower = jnp.linalg.cholesky(gram)  68.6 us
    another operation x5, other arithmetic, solve_rows(): return jax.scipy.linalg.cho_solve((lower, True), rows.T).T  39.4 us
  transfers between devices with their start and end apart: 6, of which 4 were waited for; matrix products, arithmetic and copies ran while one was open for 22% of the time, Pallas kernels for 0%

commit v1 on v0

--- a/solution.py
+++ b/solution.py
@@ -2,6 +2,7 @@
 import jax.numpy as jnp
 from jax import lax
 from jax.sharding import PartitionSpec as P
+from jax.lax import psum
 
 EPS = 1e-06
 
@@ -108,7 +109,9 @@
     system_one = gram_b * gram_c
     summed_own = lax.psum_scatter(stored_one, ("ja", "ka"), scatter_dimension=0, tiled=True)
     a_hat = solve_rows(system_one, summed_own)
-    squares_a = lax.psum(jnp.sum(a_hat * a_hat, axis=0), ("ia", "ja", "ka"))
+    squares_a = jnp.sum(a_hat * a_hat, axis=0)
+    for k in ("ia", ("ja", "ka")):
+        squares_a = psum(squares_a, k)
     scale_a = jnp.sqrt(squares_a / total_one + EPS)
     a_own = a_hat / scale_a
     local_a = jnp.dot(a_own.T, a_own, precision=highest, preferred_element_type=jnp.float32)

time: 837 us -> 881 us (1.053)
  blocking collectives: 155 us -> 214 us
  loops' own time: 12.2 us -> 1.74 us
    psum x1 -> x2, blocking collectives: 77.9 us -> 136 us  [body(): squares_a = psum(squares_a, k)]
    another operation x2, loops' own time: 10.9 us -> 0.53 us  [solve_rows(): return jax.scipy.linalg.cho_solve((lower, True), rows.T).T]
  transfers between devices with their start and end apart: 6 -> 6, of which waited for: 4 -> 4; matrix products, arithmetic and copies ran while one was open for 22% -> 21% of each run, Pallas kernels for 0% -> 0%
where the time goes in v1:
time: 881 us; the launch traced here: 872 us
  waiting for transfers between devices  444 us (50%)
  blocking collectives  214 us (24%)
  other arithmetic  133 us (15%)
  local copies, waits for them, and re-layouts  42.5 us (5%)
  between operations  19.3 us (2%)
  matrix products  17.4 us (2%)
    psum x1, waiting for transfers between devices, body(): gram_a = lax.psum(local_a, ('ia', 'ja', 'ka'))  150 us
    psum x1, waiting for transfers between devices, body(): gram_b, gram_c = lax.psum((local_b, local_c), ('ia', 'ja', 'ka'))  149 us
    psum x2, blocking collectives, body(): squares_a = psum(squares_a, k)  136 us
    psum x1, blocking collectives, body(): squares_b = lax.psum(jnp.sum(b_hat * b_hat, axis=0), ('ia', 'ja', 'ka'))  77.7 us
    all_gather x1, waiting for transfers between devices, body(): lax.all_gather(factor_b.astype(jnp.bfloat16), ('ia', 'ka'), axis=1, tiled...  75.5 us
    all_gather x1, waiting for transfers between devices, body(): lax.all_gather(a_own.astype(jnp.bfloat16)[None], ('ja', 'ka'), axis=1, ti...  68.8 us
    another operation x13, other arithmetic, solve_rows(): lower = jnp.linalg.cholesky(gram)  68.6 us
    another operation x5, other arithmetic, solve_rows(): return jax.scipy.linalg.cho_solve((lower, True), rows.T).T  39.4 us
  transfers between devices with their start and end apart: 6, of which 4 were waited for; matrix products, arithmetic and copies ran while one was open for 21% of the time, Pallas kernels for 0%

profile of v1, /device:TPU:1, one launch (start us, length us, event | category | flops | bytes accessed | tf_op | source)
XLA Modules:
  0.0 872.1 jit_solution(7007720908364222235)
XLA Ops:
  17.5 75.5 %all-gather.4.cloned.1.call-done = bf16[1,2048,256]{2,1,0:T(8,128)(2,1)} async-done(((bf16[1,32,256]{2,1,0:T(8,128)(2,1)}), bf16[1,2048,256]{2,1,0:T(8,128)(2,1)}) %all-gather.4.cloned.1.call-update) | async-done | bytes 1048592 | tf_op jit(solution)/shard_map/all_gather | solution.py:81
  94.8 23.3 %conditional.4 = (f32[2048,256]{1,0:T(8,128)}) conditional(s32[]{:T(128)} %bitcast.41, () %tuple.54, (s32[1,1,1,2]{3,2,1,0:T(1,128)}, bf16[512,256]{1,0:T(8,128)(2,1)S(1)}, bf16[1,1,1,2,128,128,128]{6,5,4,3,2,1,0:T(8,128)(2,1)}, s32[1,1,1,2]{3,2,1,0:T(1,128)}, bf16[2048,256]{1,0:T(8,128)(2,1)S(1)}, /*index=5*/s32[1,1,1,2]{3,2,1,0:T(1,128)}) %tuple.134), branch_computations={%region_6.0_spmd, %region_7.0_spmd} | conditional | flops 1082130432 | bytes 83099928 | solution.py:105
  100.7 6.7 copy.52
  107.6 8.2 multiply_reduce_fusion
  122.3 149.3 %all-reduce.7.cloned.1.call-done = (f32[256,256]{0,1:T(8,128)}, f32[256,256]{0,1:T(8,128)}) async-done(((f32[256,256]{0,1:T(8,128)}, f32[256,256]{0,1:T(8,128)}), (f32[256,256]{0,1:T(8,128)}, f32[256,256]{0,1:T(8,128)})) %all-reduce.7.cloned.1.call-update) | async-done | bytes 524304 | tf_op jit(solution)/shard_map/psum | solution.py:80
  272.9 11.7 %cholesky.130 = f32[128,128]{1,0:T(8,128)S(1)} custom-call(f32[128,128]{1,0:T(8,128)S(1)} %cholesky.194), custom_call_target="Cholesky" | custom-call | tf_op jit(solution)/shard_map/jit(cholesky)/cholesky | solution.py:11
  284.7 9.8 %custom-call.15 = f32[1,128,128]{1,2,0:T(8,128)S(1)} custom-call(f32[1,128,128]{2,1,0:T(8,128)S(1)} %get-tuple-element.155), custom_call_target="InvertDiagBlocksLowerTriangular" | custom-call | tf_op jit(solution)/shard_map/jit(cholesky)/cholesky | solution.py:11
  295.0 11.7 %cholesky.147 = f32[128,128]{1,0:T(8,128)S(1)} custom-call(f32[128,128]{1,0:T(8,128)S(1)} %convolution_subtract_fusion.1), custom_call_target="Cholesky" | custom-call | tf_op jit(solution)/shard_map/jit(cholesky)/cholesky | solution.py:11
  308.8 4.1 while.4
  312.9 19.7 %custom-call.16 = f32[2,128,128]{1,2,0:T(8,128)S(1)} custom-call(f32[2,128,128]{2,1,0:T(8,128)S(1)} %get-tuple-element.124), custom_call_target="InvertDiagBlocksLowerTriangular" | custom-call | tf_op jit(solution)/shard_map/jit(_cho_solve)/triangular_solve | solution.py:12
  335.5 8.0 psum.44
  343.5 127.8 %psum.45 = f32[256]{0:T(256)S(1)} all-reduce(f32[256]{0:T(256)S(1)} %psum.44), channel_id=1, replica_groups=mesh['ia'=4,'ja'=4,'ka'=16] {'ja','ka'}, use_global_device_ids=true, to_apply=%region_14.17 | all-reduce | flops 256 | bytes 2048 | tf_op jit(solution)/shard_map/psum | solution.py:114
  473.3 68.8 %all-gather.6.cloned.1.call-done = bf16[2048,256]{1,0:T(8,128)(2,1)} async-done(((bf16[32,256]{1,0:T(8,128)(2,1)}), bf16[2048,256]{1,0:T(8,128)(2,1)}) %all-gather.6.cloned.1.call-update) | async-done | bytes 1048592 | tf_op jit(solution)/shard_map/all_gather | solution.py:119
  543.9 23.6 %conditional.6 = (f32[2048,256]{1,0:T(8,128)}) conditional(s32[]{:T(128)} %bitcast.41, () %tuple.57, (s32[1,1,1,2]{3,2,1,0:T(1,128)S(1)}, bf16[2048,256]{1,0:T(8,128)(2,1)S(1)}, bf16[1,1,1,2,128,128,128]{6,5,4,3,2,1,0:T(8,128)(2,1)}, s32[1,1,1,2]{3,2,1,0:T(1,128)S(1)}, bf16[512,256]{1,0:T(8,128)(2,1)S(1)}, ...), branch_computations={%region_16.19_spmd, %region_17.20_spmd} | conditional | flops 1082130432 | bytes 83099800 | solution.py:142
  550.1 6.7 copy.55
  557.0 8.3 multiply_reduce_fusion.2
  567.7 3.7 gather_fusion.3
  571.4 150.4 %all-reduce.5.cloned.1.call-done = f32[256,256]{0,1:T(8,128)} async-done(((f32[256,256]{0,1:T(8,128)}), f32[256,256]{0,1:T(8,128)}) %all-reduce.5.cloned.1.call-update) | async-done | bytes 262160 | tf_op jit(solution)/shard_map/psum | solution.py:118
  723.0 11.7 %cholesky.164 = f32[128,128]{1,0:T(8,128)S(1)} custom-call(f32[128,128]{1,0:T(8,128)S(1)} %cholesky.197), custom_call_target="Cholesky" | custom-call | tf_op jit(solution)/shard_map/jit(cholesky)/cholesky | solution.py:11
  734.8 9.8 %custom-call.17 = f32[1,128,128]{1,2,0:T(8,128)S(1)} custom-call(f32[1,128,128]{2,1,0:T(8,128)S(1)} %get-tuple-element.151), custom_call_target="InvertDiagBlocksLowerTriangular" | custom-call | tf_op jit(solution)/shard_map/jit(cholesky)/cholesky | solution.py:11
  745.1 11.7 %cholesky.181 = f32[128,128]{1,0:T(8,128)S(1)} custom-call(f32[128,128]{1,0:T(8,128)S(1)} %convolution_subtract_fusion), custom_call_target="Cholesky" | custom-call | tf_op jit(solution)/shard_map/jit(cholesky)/cholesky | solution.py:11
  759.5 4.2 while.5
  763.7 19.7 %custom-call.18 = f32[2,128,128]{1,2,0:T(8,128)S(1)} custom-call(f32[2,128,128]{2,1,0:T(8,128)S(1)} %get-tuple-element.125), custom_call_target="InvertDiagBlocksLowerTriangular" | custom-call | tf_op jit(solution)/shard_map/jit(_cho_solve)/triangular_solve | solution.py:12
  786.2 77.7 %psum.47 = f32[256]{0:T(256)S(1)} all-reduce(f32[256]{0:T(256)S(1)} %multiply_reduce_fusion.4), channel_id=1, replica_groups=mesh['ia'=4,'ja'=4,'ka'=16] {'ia','ja','ka'}, use_global_device_ids=true, to_apply=%region_23.26 | all-reduce | flops 256 | bytes 2048 | tf_op jit(solution)/shard_map/psum | solution.py:148
  (118 shorter events, 54.4 us)
Async XLA Ops:
  8.0 85.0 %all-gather.4.cloned.1.call-start = ((), (), s32[]{:S(2)}) async-start(), calls=%async_computation.2 | async-start | bytes 1064960 | tf_op jit(solution)/shard_map/all_gather | solution.py:81
  9.4 262.2 %all-reduce.7.cloned.1.call-start = ((), (), s32[]{:S(2)}) async-start(), calls=%async_computation.7 | async-start | bytes 1048576 | tf_op jit(solution)/shard_map/psum | solution.py:80
  13.5 319.2 %reduce-scatter.3.cloned.1.call-start = ((), (), s32[]{:S(2)}) async-start(), calls=%async_computation.3 | async-start | bytes 2129920 | tf_op jit(solution)/shard_map/reduce_scatter | solution.py:110
  100.7 6.7 copy-start.4
  107.5 8.4 copy-start.7
  121.7 350.3 %copy-start.1 = (s32[64]{0:T(128)S(1)}, s32[64]{0:T(128)}, u32[]{:S(2)}) copy-start(s32[64]{0:T(128)} %param.25) | copy-start | bytes 772
  121.8 420.3 %all-gather.6.cloned.1.call-start = ((), (), s32[]{:S(2)}) async-start(), calls=%async_computation.6 | async-start | bytes 1064960 | tf_op jit(solution)/shard_map/all_gather | solution.py:119
  271.6 272.3 %copy-start.2 = (s32[1,1,1,2]{3,2,1,0:T(1,128)S(1)}, s32[1,1,1,2]{3,2,1,0:T(1,128)}, u32[]{:S(2)}) copy-start(s32[1,1,1,2]{3,2,1,0:T(1,128)} %param.23) | copy-start | bytes 28
  271.6 272.3 %copy-start.3 = (s32[1,1,1,2]{3,2,1,0:T(1,128)S(1)}, s32[1,1,1,2]{3,2,1,0:T(1,128)}, u32[]{:S(2)}) copy-start(s32[1,1,1,2]{3,2,1,0:T(1,128)} %param.22) | copy-start | bytes 28
  271.6 272.3 %copy-start.6 = (s32[1,1,1,2]{3,2,1,0:T(1,128)S(1)}, s32[1,1,1,2]{3,2,1,0:T(1,128)}, u32[]{:S(2)}) copy-start(s32[1,1,1,2]{3,2,1,0:T(1,128)} %param.21) | copy-start | bytes 28
  471.9 249.9 %all-reduce.5.cloned.1.call-start = ((), (), s32[]{:S(2)}) async-start(), calls=%async_computation.4 | async-start | bytes 524288 | tf_op jit(solution)/shard_map/psum | solution.py:118
  473.2 310.2 %reduce-scatter.5.cloned.1.call-start = ((), (), s32[]{:S(2)}) async-start(), calls=%async_computation.5 | async-start | bytes 2129920 | tf_op jit(solution)/shard_map/reduce_scatter | solution.py:146
  567.7 154.1 %copy-start = (f32[256,256]{0,1:T(8,128)S(1)}, f32[256,256]{0,1:T(8,128)}, u32[]{:S(2)}) copy-start(f32[256,256]{0,1:T(8,128)} %get-tuple-element.143) | copy-start | bytes 786436
Sparse Core Ops, SparseCore 0:
  12.2 80.7 all-gather.3
  121.9 159.1 reduce-scatter.2
  472.1 69.9 all-gather.5
  571.5 159.6 reduce-scatter.4
Sparse Core Ops, SparseCore 1:
  15.6 256.0 all-reduce.6
  478.8 243.0 all-reduce.4
